TPU v7x, 256 devices: a whole 4x4x8 slice. The times are simulated.
256 devices in a mesh: row: 16 (over z, core), col: 8 (over x_hi, y), feat: 2 (over x_lo).
Axes of the slice: x: 4 (x_hi: 2, x_lo: 2; x = x_hi * 2 + x_lo), y: 4, z: 8, core: 2. Of those that a mesh axis runs over, the one named last changes fastest.
Arguments:
- features: bfloat16 [65536, 256], P(('col', 'row'), 'feat'), may hold values from -6 to 6
- tile_rows: int32 [16, 8, 256], P('row', 'col'), may hold values from 0 to 31, as said below
- tile_cols: int32 [16, 8, 256], P('row', 'col'), may hold values from 0 to 63
- tile_count: int32 [16, 8], P('row', 'col'), may hold values from 64 to 256, as said below
- tile_values: bfloat16 [16, 8, 256, 128, 128], P('row', 'col'), may hold values from -0.21875 to 0.21875
- weights: bfloat16 [256, 256], replicated, may hold values from -0.375 to 0.375
- cotangent: bfloat16 [65536, 256], P(('row', 'col'), 'feat'), may hold values from -6 to 6
Outputs:
- activated: bfloat16 [65536, 256], P(('row', 'col'), 'feat')
- feature_grad: bfloat16 [65536, 256], P(('col', 'row'), 'feat')
- weight_grad: float32 [256, 256], P('feat')
Inputs may be any that keep to these rules, and one draw needn't show every extreme that they name: `tile_rows`: block rows of a cell, unevenly loaded. `tile_count`: some cell has all 256 slots live.
All inputs are finite; a program needn't handle non-finite values.
Results may differ from a plain program's by a relative error of at most 0.027.
Values may be sent and summed in bfloat16 or wider, within the bound.
A program may use at most 128 MiB of HBM per device.

v0:
```python
import jax
import jax.numpy as jnp
from jax import lax
from jax.sharding import PartitionSpec as P


def shards(features, tile_rows, tile_cols, tile_count, tile_values, weights, cotangent):
    width = tile_values.shape[-1]
    slots = tile_values.shape[2]
    local_tiles = tile_values[0, 0]
    block_rows = tile_rows[0, 0]
    block_cols = tile_cols[0, 0]
    live_mask = (jnp.arange(slots) < tile_count[0, 0]).astype(jnp.float32)
    n_rowdev = lax.axis_size("row")
    n_coldev = lax.axis_size("col")
    local_blocks = features.shape[0] // width
    feat_half = features.shape[1]
    feat_index = lax.axis_index("feat")
    row_blocks = local_blocks * n_coldev
    col_blocks = local_blocks * n_rowdev
    node_total = features.shape[0] * n_rowdev * n_coldev
    panel = lax.all_gather(features, "row", axis=0, tiled=True)
    gathered = panel.reshape(col_blocks, width, feat_half)[block_cols]
    products = jnp.einsum("tij,tjf->tif", local_tiles, gathered, preferred_element_type=jnp.float32)
    products = products * live_mask[:, None, None]
    partial_value = (
        jnp.zeros((row_blocks, width, feat_half), jnp.float32).at[block_rows].add(products)
    )
    summed = lax.psum_scatter(
        partial_value.reshape(row_blocks * width, feat_half).astype(jnp.bfloat16),
        "col",
        scatter_dimension=0,
        tiled=True,
    )
    weight_rows = lax.dynamic_slice_in_dim(weights, feat_index * feat_half, feat_half, 0)
    mix_term = jnp.dot(summed, weight_rows, preferred_element_type=jnp.float32)
    hidden = lax.psum_scatter(
        mix_term.astype(jnp.bfloat16), "feat", scatter_dimension=1, tiled=True
    ).astype(jnp.float32)
    negative = jnp.minimum(hidden, 0.0)
    activated = jnp.where(hidden > 0, hidden, jnp.expm1(negative)).astype(jnp.bfloat16)
    slope_factor = jnp.where(hidden > 0, 1.0, jnp.exp(negative))
    grad_out = (cotangent.astype(jnp.float32) * slope_factor).astype(jnp.bfloat16)
    grad_whole = lax.all_gather(grad_out, "feat", axis=1, tiled=True)
    weight_term = lax.dot_general(
        summed, grad_whole, (((0,), (0,)), ((), ())), preferred_element_type=jnp.float32
    )
    n_feat = lax.axis_size("feat")
    slots = jnp.zeros((n_feat,) + weight_term.shape, jnp.float32)
    slots = lax.dynamic_update_slice_in_dim(slots, weight_term[None], feat_index, 0)
    slots = lax.psum(slots, ("row", "col", "feat"))
    weight_grad = lax.dynamic_index_in_dim(slots, feat_index, 0, keepdims=False) * node_total ** (
        -0.5
    )
    spread = lax.dot_general(
        grad_whole, weight_rows, (((1,), (1,)), ((), ())), preferred_element_type=jnp.float32
    ).astype(jnp.bfloat16)
    spread_panel = lax.all_gather(spread, "col", axis=0, tiled=True)
    spread_blocks = spread_panel.reshape(row_blocks, width, feat_half)[block_rows]
    back_products = jnp.einsum(
        "tji,tjf->tif", local_tiles, spread_blocks, preferred_element_type=jnp.float32
    )
    back_products = back_products * live_mask[:, None, None]
    back_partial = (
        jnp.zeros((col_blocks, width, feat_half), jnp.float32).at[block_cols].add(back_products)
    )
    back_summed = lax.psum_scatter(
        back_partial.reshape(col_blocks * width, feat_half).astype(jnp.bfloat16),
        "row",
        scatter_dimension=0,
        tiled=True,
    )
    return (activated, back_summed, weight_grad)


def solution(mesh):
    return jax.shard_map(
        shards,
        mesh=mesh,
        in_specs=(
            P(("col", "row"), "feat"),
            P("row", "col", None),
            P("row", "col", None),
            P("row", "col"),
            P("row", "col", None, None, None),
            P(),
            P(("row", "col"), "feat"),
        ),
        out_specs=(P(("row", "col"), "feat"), P(("col", "row"), "feat"), P("feat", None)),
        check_vma=False,
    )
```

profile of v0, /device:TPU:2, one launch (start us, length us, event | category | flops | bytes accessed | tf_op | source)
XLA Modules:
  0.0 605.1 jit_solution(15216501221385841070)
XLA Ops:
  7.2 0.0 copy-start
  7.2 0.0 all-gather.3.cloned.1.call-start
  7.2 0.7 all-gather.3.cloned.1.call-update
  7.9 0.0 reduce-scatter.6.cloned.1.call-start
  8.6 0.7 compare_select_fusion
  9.3 43.2 %all-gather.3.cloned.1.call-done = bf16[8192,128]{1,0:T(8,128)(2,1)} async-done(((bf16[512,128]{1,0:T(8,128)(2,1)}), bf16[8192,128]{1,0:T(8,128)(2,1)}) %all-gather.3.cloned.1.call-update) | async-done | bytes 2097168 | tf_op jit(solution)/shard_map/all_gather | solution.py:22
  52.6 10.2 %gather_fusion = bf16[256,128,128]{2,1,0:T(8,128)(2,1)} fusion(bf16[64,128,128]{2,1,0:T(8,128)(2,1)} %bitcast.36, s32[1024]{0:T(1024)S(1)} %pad_clamp_fusion.1), kind=kCustom, calls=%fused_computation | custom fusion | bytes 16778240 | tf_op jit(solution)/shard_map/gather | solution.py:23
  62.8 13.0 %multiply_bitcast_fusion.1 = f32[256,128,128]{1,2,0:T(8,128)} fusion(bf16[256,128,128]{2,1,0:T(8,128)(2,1)} %gather_fusion, bf16[1,1,256,128,128]{4,3,2,1,0:T(8,128)(2,1)} %param.11, f32[256]{0:T(256)S(1)} %compare_convert_fusion), kind=kOutput, calls=%fused_computation.5 | convolution fusion | flops 1077936128 | bytes 33555456 | tf_op jit(solution)/shard_map/tij,tjf->tif/dot_general | solution.py:24
  75.8 17.4 %copy.17 = f32[256,128,128]{2,1,0:T(8,128)} copy(f32[256,128,128]{1,2,0:T(8,128)} %multiply_bitcast_fusion.1) | data formatting | bytes 33554432 | tf_op jit(solution)/shard_map/mul | solution.py:25
  93.2 0.2 broadcast_in_dim.22
  93.5 0.0 copy-start.3
  93.5 33.2 %scatter_fusion = f32[32,128,128]{2,1,0:T(8,128)S(1)} fusion(f32[32,128,128]{2,1,0:T(8,128)S(1)} %broadcast_in_dim.22, s32[256]{0:T(256)S(1)} %bitcast.43, f32[256,128,128]{2,1,0:T(8,128)} %copy.17), kind=kCustom, calls=%fused_computation.2 | custom fusion | flops 4194304 | bytes 50332672 | tf_op jit(solution)/shard_map/scatter-add | solution.py:27
  126.7 1.1 convert_element_type.38
  127.8 0.0 reduce-scatter.6.cloned.1.call-update
  127.8 0.0 reduce-scatter.10.cloned.1.call-start
  127.9 74.5 %reduce-scatter.6.cloned.1.call-done = bf16[512,128]{1,0:T(8,128)(2,1)} async-done(((bf16[4096,128]{1,0:T(8,128)(2,1)}), bf16[512,128]{1,0:T(8,128)(2,1)}) %reduce-scatter.6.cloned.1.call-update) | async-done | bytes 131088 | tf_op jit(solution)/shard_map/reduce_scatter | solution.py:29
  202.3 0.0 copy-done
  202.4 1.1 convolution_convert_fusion
  203.5 0.8 copy.22
  204.3 0.0 reduce-scatter.10.cloned.1.call-update
  204.3 0.0 all-gather.5.cloned.1.call-start
  204.4 16.0 %reduce-scatter.10.cloned.1.call-done = bf16[128,512]{1,0:T(8,128)(2,1)} async-done(((bf16[256,512]{1,0:T(8,128)(2,1)}), bf16[128,512]{1,0:T(8,128)(2,1)}) %reduce-scatter.10.cloned.1.call-update) | async-done | bytes 131088
  220.4 1.0 copy.23
  221.4 0.0 copy-done.3
  221.5 0.8 fusion.7
  222.3 5.9 all_gather.10
  228.2 0.9 convolution_convert_fusion.1
  229.0 0.0 all-gather.5.cloned.1.call-update
  229.1 0.0 all-reduce.2.cloned.1.call-start
  229.2 1.1 fusion.2
  230.3 0.0 copy-start.2
  230.3 0.7 copy-done.2
  231.0 0.0 all-reduce.2.cloned.1.call-update
  231.0 0.2 reduce-scatter.8.cloned.1.call-start
  231.3 50.6 %all-gather.5.cloned.1.call-done = bf16[4096,128]{1,0:T(8,128)(2,1)} async-done(((bf16[512,128]{1,0:T(8,128)(2,1)}), bf16[4096,128]{1,0:T(8,128)(2,1)}) %all-gather.5.cloned.1.call-update) | async-done | bytes 1048592 | tf_op jit(solution)/shard_map/all_gather | solution.py:58
  281.9 9.8 %gather_fusion.1 = bf16[256,128,128]{2,1,0:T(8,128)(2,1)} fusion(bf16[32,128,128]{2,1,0:T(8,128)(2,1)} %bitcast.35, s32[1024]{0:T(1024)S(1)} %pad_clamp_fusion), kind=kCustom, calls=%fused_computation.1 | custom fusion | bytes 16778240 | tf_op jit(solution)/shard_map/gather | solution.py:59
  291.7 15.4 %multiply_bitcast_fusion = f32[256,128,128]{1,2,0:T(8,128)} fusion(bf16[256,128,128]{2,1,0:T(8,128)(2,1)} %gather_fusion.1, bf16[1,1,256,128,128]{4,3,2,1,0:T(8,128)(2,1)} %param.11, f32[256]{0:T(256)S(1)} %compare_convert_fusion), kind=kOutput, calls=%fused_computation.4 | convolution fusion | flops 1077936128 | bytes 33555456 | tf_op jit(solution)/shard_map/tji,tjf->tif/dot_general | solution.py:60
  307.1 17.5 %copy.19 = f32[256,128,128]{2,1,0:T(8,128)} copy(f32[256,128,128]{1,2,0:T(8,128)} %multiply_bitcast_fusion) | data formatting | bytes 33554432 | tf_op jit(solution)/shard_map/mul | solution.py:63
  324.6 2.5 broadcast_in_dim.23
  327.0 0.0 copy-start.1
  327.0 52.1 %scatter_fusion.1 = f32[64,128,128]{2,1,0:T(8,128)} fusion(f32[64,128,128]{2,1,0:T(8,128)} %broadcast_in_dim.23, s32[256]{0:T(256)S(1)} %bitcast.42, f32[256,128,128]{2,1,0:T(8,128)} %copy.19), kind=kCustom, calls=%fused_computation.3 | custom fusion | flops 4194304 | bytes 50332672 | tf_op jit(solution)/shard_map/scatter-add | solution.py:65
  379.1 3.9 convert_element_type.46
  383.0 0.0 reduce-scatter.8.cloned.1.call-update
  383.1 154.2 %all-reduce.2.cloned.1.call-done = f32[2,128,256]{2,1,0:T(8,128)} async-done(((f32[2,128,256]{2,1,0:T(8,128)}), f32[2,128,256]{2,1,0:T(8,128)}) %all-reduce.2.cloned.1.call-update) | async-done | bytes 262160 | tf_op jit(solution)/shard_map/psum | solution.py:51
  537.3 1.6 multiply_bitcast_fusion.2
  538.8 59.4 %reduce-scatter.8.cloned.1.call-done = bf16[512,128]{1,0:T(8,128)(2,1)} async-done(((bf16[8192,128]{1,0:T(8,128)(2,1)}), bf16[512,128]{1,0:T(8,128)(2,1)}) %reduce-scatter.8.cloned.1.call-update) | async-done | bytes 131088 | tf_op jit(solution)/shard_map/reduce_scatter | solution.py:67
  598.3 0.0 copy-done.1
  (4 shorter events, 0.0 us)
Async XLA Ops:
  7.2 195.2 %copy-start = (bf16[256,256]{1,0:T(8,128)(2,1)S(1)}, bf16[256,256]{1,0:T(8,128)(2,1)}, u32[]{:S(2)}) copy-start(bf16[256,256]{1,0:T(8,128)(2,1)} %param.12) | copy-start | bytes 393220
  7.2 45.4 %all-gather.3.cloned.1.call-start = ((), (), s32[]{:S(2)}) async-start(), calls=%async_computation.3 | async-start | bytes 2228224 | tf_op jit(solution)/shard_map/all_gather | solution.py:22
  7.9 194.4 %reduce-scatter.6.cloned.1.call-start = ((), (), s32[]{:S(2)}) async-start(), calls=%async_computation.4 | async-start | bytes 1179648 | tf_op jit(solution)/shard_map/reduce_scatter | solution.py:29
  93.5 128.0 %copy-start.3 = (bf16[512,128]{1,0:T(8,128)(2,1)S(1)}, bf16[512,128]{1,0:T(8,128)(2,1)}, u32[]{:S(2)}) copy-start(bf16[512,128]{1,0:T(8,128)(2,1)} %param.13) | copy-start | bytes 393220
  127.8 92.6 %reduce-scatter.10.cloned.1.call-start = ((), (), s32[]{:S(2)}) async-start(), calls=%async_computation.8 | async-start | bytes 393216
  204.3 77.5 %all-gather.5.cloned.1.call-start = ((), (), s32[]{:S(2)}) async-start(), calls=%async_computation.5 | async-start | bytes 1179648 | tf_op jit(solution)/shard_map/all_gather | solution.py:58
  229.1 308.2 %all-reduce.2.cloned.1.call-start = ((), (), s32[]{:S(2)}) async-start(), calls=%async_computation.7 | async-start | bytes 524288 | tf_op jit(solution)/shard_map/psum | solution.py:51
  230.3 0.7 copy-start.2
  231.0 367.2 %reduce-scatter.8.cloned.1.call-start = ((), (), s32[]{:S(2)}) async-start(), calls=%async_computation.6 | async-start | bytes 2228224 | tf_op jit(solution)/shard_map/reduce_scatter | solution.py:67
  327.0 271.2 %copy-start.1 = (bf16[256,256]{1,0:T(8,128)(2,1)S(1)}, bf16[256,256]{1,0:T(8,128)(2,1)}, u32[]{:S(2)}) copy-start(bf16[256,256]{1,0:T(8,128)(2,1)} %param.12) | copy-start | bytes 393220
Sparse Core Ops, SparseCore 0:
  9.8 42.6 all-gather.2
  127.9 74.3 reduce-scatter.5
  205.0 15.3 reduce-scatter.9
  229.2 52.6 all-gather.4
  287.2 250.0 all-reduce.1
  540.2 57.9 reduce-scatter.7
where the time goes:
time: 607 us; the launch traced here: 605 us
  waiting for transfers between devices  399 us (66%)
  other arithmetic  93.4 us (15%)
  local copies, waits for them, and re-layouts  60.2 us (10%)
  matrix products  31.5 us (5%)
  between operations  14.9 us (2%)
    psum x1, waiting for transfers between devices, shards(): slots = lax.psum(slots, ('row', 'col', 'feat'))  154 us
    reduce_scatter x1, waiting for transfers between devices, shards(): lax.psum_scatter(partial_value.reshape(row_blocks * width, feat_half).ast...  74.5 us
    reduce_scatter x1, waiting for transfers between devices, shards(): lax.psum_scatter(back_partial.reshape(col_blocks * width, feat_half).asty...  59.4 us
    scatter-add x1, other arithmetic, shards(): jnp.zeros((col_blocks, width, feat_half), jnp.float32).at[block_cols]  52.1 us
    all_gather x1, waiting for transfers between devices, shards(): spread_panel = lax.all_gather(spread, 'col', axis=0, tiled=True)  50.6 us
    all_gather x1, waiting for transfers between devices, shards(): panel = lax.all_gather(features, 'row', axis=0, tiled=True)  43.2 us
    scatter-add x1, other arithmetic, shards(): jnp.zeros((row_blocks, width, feat_half), jnp.float32).at[block_rows]  33.2 us
    mul x1, local copies, waits for them, and re-layouts, shards(): back_products = back_products * live_mask[:, None, None]  17.5 us
  transfers between devices with their start and end apart: 6, of which 6 were waited for; matrix products, arithmetic and copies ran while one was open for 17% of the time, Pallas kernels for 0%

commit v1 on v0

--- a/solution.py
+++ b/solution.py
@@ -48,7 +48,7 @@
     n_feat = lax.axis_size("feat")
     slots = jnp.zeros((n_feat,) + weight_term.shape, jnp.float32)
     slots = lax.dynamic_update_slice_in_dim(slots, weight_term[None], feat_index, 0)
-    slots = lax.psum(slots, ("row", "col", "feat"))
+    slots = lax.psum(lax.psum(slots, ("col", "feat")), "row")
     weight_grad = lax.dynamic_index_in_dim(slots, feat_index, 0, keepdims=False) * node_total ** (
         -0.5
     )

time: 607 us -> 562 us (0.926)
  waiting for transfers between devices: 399 us -> 354 us
    psum x1 -> x2, waiting for transfers between devices: 154 us -> 105 us  [shards(): slots = lax.psum(lax.psum(slots, ('col', 'feat')), 'row')]
    unnamed x7 -> x8, waiting for transfers between devices: 16.8 us -> 16.8 us
  transfers between devices with their start and end apart: 6 -> 7, of which waited for: 6 -> 7; matrix products, arithmetic and copies ran while one was open for 17% -> 19% of each run, Pallas kernels for 0% -> 0%
where the time goes in v1:
time: 562 us; the launch traced here: 560 us
  waiting for transfers between devices  354 us (63%)
  other arithmetic  93.4 us (17%)
  local copies, waits for them, and re-layouts  60.2 us (11%)
  matrix products  31.6 us (6%)
  between operations  14.9 us (3%)
  blocking collectives  5.89 us (1%)
    psum x2, waiting for transfers between devices, shards(): slots = lax.psum(lax.psum(slots, ('col', 'feat')), 'row')  105 us
    reduce_scatter x1, waiting for transfers between devices, shards(): lax.psum_scatter(partial_value.reshape(row_blocks * width, feat_half).ast...  74.5 us
    reduce_scatter x1, waiting for transfers between devices, shards(): lax.psum_scatter(back_partial.reshape(col_blocks * width, feat_half).asty...  61.1 us
    all_gather x1, waiting for transfers between devices, shards(): spread_panel = lax.all_gather(spread, 'col', axis=0, tiled=True)  53.5 us
    scatter-add x1, other arithmetic, shards(): jnp.zeros((col_blocks, width, feat_half), jnp.float32).at[block_cols]  52 us
    all_gather x1, waiting for transfers between devices, shards(): panel = lax.all_gather(features, 'row', axis=0, tiled=True)  43.2 us
    scatter-add x1, other arithmetic, shards(): jnp.zeros((row_blocks, width, feat_half), jnp.float32).at[block_rows]  33.2 us
    mul x1, local copies, waits for them, and re-layouts, shards(): back_products = back_products * live_mask[:, None, None]  17.5 us
  transfers between devices with their start and end apart: 7, of which 7 were waited for; matrix products, arithmetic and copies ran while one was open for 19% of the time, Pallas kernels for 0%

profile of v1, /device:TPU:2, one launch (start us, length us, event | category | flops | bytes accessed | tf_op | source)
XLA Modules:
  0.0 560.2 jit_solution(625113207653389168)
XLA Ops:
  7.2 0.0 copy-start
  7.2 0.0 all-gather.3.cloned.1.call-start
  7.2 0.7 all-gather.3.cloned.1.call-update
  7.9 0.0 reduce-scatter.6.cloned.1.call-start
  8.6 0.7 compare_select_fusion
  9.3 43.2 %all-gather.3.cloned.1.call-done = bf16[8192,128]{1,0:T(8,128)(2,1)} async-done(((bf16[512,128]{1,0:T(8,128)(2,1)}), bf16[8192,128]{1,0:T(8,128)(2,1)}) %all-gather.3.cloned.1.call-update) | async-done | bytes 2097168 | tf_op jit(solution)/shard_map/all_gather | solution.py:22
  52.6 10.2 %gather_fusion = bf16[256,128,128]{2,1,0:T(8,128)(2,1)} fusion(bf16[64,128,128]{2,1,0:T(8,128)(2,1)} %bitcast.36, s32[1024]{0:T(1024)S(1)} %pad_clamp_fusion.1), kind=kCustom, calls=%fused_computation | custom fusion | bytes 16778240 | tf_op jit(solution)/shard_map/gather | solution.py:23
  62.8 13.0 %multiply_bitcast_fusion.1 = f32[256,128,128]{1,2,0:T(8,128)} fusion(bf16[256,128,128]{2,1,0:T(8,128)(2,1)} %gather_fusion, bf16[1,1,256,128,128]{4,3,2,1,0:T(8,128)(2,1)} %param.11, f32[256]{0:T(256)S(1)} %compare_convert_fusion), kind=kOutput, calls=%fused_computation.5 | convolution fusion | flops 1077936128 | bytes 33555456 | tf_op jit(solution)/shard_map/tij,tjf->tif/dot_general | solution.py:24
  75.8 17.4 %copy.17 = f32[256,128,128]{2,1,0:T(8,128)} copy(f32[256,128,128]{1,2,0:T(8,128)} %multiply_bitcast_fusion.1) | data formatting | bytes 33554432 | tf_op jit(solution)/shard_map/mul | solution.py:25
  93.2 0.2 broadcast_in_dim.22
  93.5 0.0 copy-start.3
  93.5 33.2 %scatter_fusion = f32[32,128,128]{2,1,0:T(8,128)S(1)} fusion(f32[32,128,128]{2,1,0:T(8,128)S(1)} %broadcast_in_dim.22, s32[256]{0:T(256)S(1)} %bitcast.43, f32[256,128,128]{2,1,0:T(8,128)} %copy.17), kind=kCustom, calls=%fused_computation.2 | custom fusion | flops 4194304 | bytes 50332672 | tf_op jit(solution)/shard_map/scatter-add | solution.py:27
  126.7 1.1 convert_element_type.38
  127.8 0.0 reduce-scatter.6.cloned.1.call-update
  127.8 0.0 reduce-scatter.10.cloned.1.call-start
  127.9 74.5 %reduce-scatter.6.cloned.1.call-done = bf16[512,128]{1,0:T(8,128)(2,1)} async-done(((bf16[4096,128]{1,0:T(8,128)(2,1)}), bf16[512,128]{1,0:T(8,128)(2,1)}) %reduce-scatter.6.cloned.1.call-update) | async-done | bytes 131088 | tf_op jit(solution)/shard_map/reduce_scatter | solution.py:29
  202.3 0.0 copy-done
  202.4 1.1 convolution_convert_fusion
  203.5 0.8 copy.22
  204.3 0.0 reduce-scatter.10.cloned.1.call-update
  204.3 0.0 all-reduce.3.cloned.1.call-start
  204.4 16.0 %reduce-scatter.10.cloned.1.call-done = bf16[128,512]{1,0:T(8,128)(2,1)} async-done(((bf16[256,512]{1,0:T(8,128)(2,1)}), bf16[128,512]{1,0:T(8,128)(2,1)}) %reduce-scatter.10.cloned.1.call-update) | async-done | bytes 131088
  220.4 1.0 copy.23
  221.4 0.0 copy-done.3
  221.5 0.8 fusion.7
  222.3 5.9 %all_gather.10 = bf16[512,256]{1,0:T(8,128)(2,1)S(1)} all-gather(bf16[512,128]{1,0:T(8,128)(2,1)S(1)} %get-tuple-element.3), channel_id=1, replica_groups=mesh['row'=16,'col'=8,'feat'=2] {'feat'}, dimensions={1}, use_global_device_ids=true | all-gather | bytes 393216 | tf_op jit(solution)/shard_map/all_gather | solution.py:44
  228.2 1.1 fusion.2
  229.3 0.0 copy-start.2
  229.3 0.7 copy-done.2
  230.0 0.0 all-reduce.3.cloned.1.call-update
  230.0 0.0 all-gather.5.cloned.1.call-start
  230.1 0.9 convolution_convert_fusion.1
  231.0 0.0 all-gather.5.cloned.1.call-update
  231.0 0.0 all-reduce.5.cloned.1.call-start
  231.1 95.3 %all-reduce.3.cloned.1.call-done = f32[2,128,256]{2,1,0:T(8,128)} async-done(((f32[2,128,256]{2,1,0:T(8,128)}), f32[2,128,256]{2,1,0:T(8,128)}) %all-reduce.3.cloned.1.call-update) | async-done | bytes 262160 | tf_op jit(solution)/shard_map/psum | solution.py:51
  326.4 0.0 all-reduce.5.cloned.1.call-update
  326.4 0.2 reduce-scatter.8.cloned.1.call-start
  326.6 53.5 %all-gather.5.cloned.1.call-done = bf16[4096,128]{1,0:T(8,128)(2,1)} async-done(((bf16[512,128]{1,0:T(8,128)(2,1)}), bf16[4096,128]{1,0:T(8,128)(2,1)}) %all-gather.5.cloned.1.call-update) | async-done | bytes 1048592 | tf_op jit(solution)/shard_map/all_gather | solution.py:58
  380.1 9.8 %gather_fusion.1 = bf16[256,128,128]{2,1,0:T(8,128)(2,1)} fusion(bf16[32,128,128]{2,1,0:T(8,128)(2,1)} %bitcast.35, s32[1024]{0:T(1024)S(1)} %pad_clamp_fusion), kind=kCustom, calls=%fused_computation.1 | custom fusion | bytes 16778240 | tf_op jit(solution)/shard_map/gather | solution.py:59
  389.9 15.4 %multiply_bitcast_fusion = f32[256,128,128]{1,2,0:T(8,128)} fusion(bf16[256,128,128]{2,1,0:T(8,128)(2,1)} %gather_fusion.1, bf16[1,1,256,128,128]{4,3,2,1,0:T(8,128)(2,1)} %param.11, f32[256]{0:T(256)S(1)} %compare_convert_fusion), kind=kOutput, calls=%fused_computation.4 | convolution fusion | flops 1077936128 | bytes 33555456 | tf_op jit(solution)/shard_map/tji,tjf->tif/dot_general | solution.py:60
  405.3 17.5 %copy.19 = f32[256,128,128]{2,1,0:T(8,128)} copy(f32[256,128,128]{1,2,0:T(8,128)} %multiply_bitcast_fusion) | data formatting | bytes 33554432 | tf_op jit(solution)/shard_map/mul | solution.py:63
  422.8 2.5 broadcast_in_dim.23
  425.3 0.0 copy-start.1
  425.3 52.0 %scatter_fusion.1 = f32[64,128,128]{2,1,0:T(8,128)} fusion(f32[64,128,128]{2,1,0:T(8,128)} %broadcast_in_dim.23, s32[256]{0:T(256)S(1)} %bitcast.42, f32[256,128,128]{2,1,0:T(8,128)} %copy.19), kind=kCustom, calls=%fused_computation.3 | custom fusion | flops 4194304 | bytes 50332672 | tf_op jit(solution)/shard_map/scatter-add | solution.py:65
  477.3 3.9 convert_element_type.46
  481.2 0.0 reduce-scatter.8.cloned.1.call-update
  481.2 9.4 %all-reduce.5.cloned.1.call-done = f32[2,128,256]{2,1,0:T(8,128)} async-done(((f32[2,128,256]{2,1,0:T(8,128)}), f32[2,128,256]{2,1,0:T(8,128)}) %all-reduce.5.cloned.1.call-update) | async-done | bytes 262160 | tf_op jit(solution)/shard_map/psum | solution.py:51
  490.7 1.6 multiply_bitcast_fusion.2
  492.2 61.1 %reduce-scatter.8.cloned.1.call-done = bf16[512,128]{1,0:T(8,128)(2,1)} async-done(((bf16[8192,128]{1,0:T(8,128)(2,1)}), bf16[512,128]{1,0:T(8,128)(2,1)}) %reduce-scatter.8.cloned.1.call-update) | async-done | bytes 131088 | tf_op jit(solution)/shard_map/reduce_scatter | solution.py:67
  553.3 0.0 copy-done.1
  (4 shorter events, 0.0 us)
Async XLA Ops:
  7.2 195.2 %copy-start = (bf16[256,256]{1,0:T(8,128)(2,1)S(1)}, bf16[256,256]{1,0:T(8,128)(2,1)}, u32[]{:S(2)}) copy-start(bf16[256,256]{1,0:T(8,128)(2,1)} %param.12) | copy-start | bytes 393220
  7.2 45.4 %all-gather.3.cloned.1.call-start = ((), (), s32[]{:S(2)}) async-start(), calls=%async_computation.3 | async-start | bytes 2228224 | tf_op jit(solution)/shard_map/all_gather | solution.py:22
  7.9 194.4 %reduce-scatter.6.cloned.1.call-start = ((), (), s32[]{:S(2)}) async-start(), calls=%async_computation.4 | async-start | bytes 1179648 | tf_op jit(solution)/shard_map/reduce_scatter | solution.py:29
  93.5 128.0 %copy-start.3 = (bf16[512,128]{1,0:T(8,128)(2,1)S(1)}, bf16[512,128]{1,0:T(8,128)(2,1)}, u32[]{:S(2)}) copy-start(bf16[512,128]{1,0:T(8,128)(2,1)} %param.13) | copy-start | bytes 393220
  127.8 92.6 %reduce-scatter.10.cloned.1.call-start = ((), (), s32[]{:S(2)}) async-start(), calls=%async_computation.9 | async-start | bytes 393216
  204.3 122.0 %all-reduce.3.cloned.1.call-start = ((), (), s32[]{:S(2)}) async-start(), calls=%async_computation.7 | async-start | bytes 524288 | tf_op jit(solution)/shard_map/psum | solution.py:51
  229.3 0.7 copy-start.2
  230.0 150.0 %all-gather.5.cloned.1.call-start = ((), (), s32[]{:S(2)}) async-start(), calls=%async_computation.5 | async-start | bytes 1179648 | tf_op jit(solution)/shard_map/all_gather | solution.py:58
  231.0 259.6 %all-reduce.5.cloned.1.call-start = ((), (), s32[]{:S(2)}) async-start(), calls=%async_computation.8 | async-start | bytes 524288 | tf_op jit(solution)/shard_map/psum | solution.py:51
  326.4 226.9 %reduce-scatter.8.cloned.1.call-start = ((), (), s32[]{:S(2)}) async-start(), calls=%async_computation.6 | async-start | bytes 2228224 | tf_op jit(solution)/shard_map/reduce_scatter | solution.py:67
  425.3 128.0 %copy-start.1 = (bf16[256,256]{1,0:T(8,128)(2,1)S(1)}, bf16[256,256]{1,0:T(8,128)(2,1)}, u32[]{:S(2)}) copy-start(bf16[256,256]{1,0:T(8,128)(2,1)} %param.12) | copy-start | bytes 393220
Sparse Core Ops, SparseCore 0:
  9.8 42.6 all-gather.2
  127.9 74.3 reduce-scatter.5
  205.0 15.3 reduce-scatter.9
  230.2 96.1 all-reduce.2
  329.8 50.2 all-gather.4
  382.4 108.2 all-reduce.4
  493.8 59.5 reduce-scatter.7
